TPU v7x, 32 devices: a whole 2x2x4 slice. The times are simulated.
32 devices in a mesh: gx: 4 (over z), gy: 8 (over y, x, core).
Axes of the slice: x: 2, y: 2, z: 4, core: 2. Of those that a mesh axis runs over, the one named last changes fastest.
Arguments:
- forcing: float32 [16, 128, 512], P(None, 'gy', 'gx'), may hold values from -6 to 6
- pressure_in: float32 [16, 128, 512], P(None, 'gy', 'gx'), may hold values from -6 to 6
- x_coupling: float32 [16, 128, 512], P(None, 'gy', 'gx'), may hold values from 0.5 to 2000
- y_coupling: float32 [16, 128, 512], P(None, 'gy', 'gx'), may hold values from 0.5 to 2000
- z_coupling: float32 [16, 128, 512], P(None, 'gy', 'gx'), may hold values from 0.05 to 0.5
- damping: float32 [16, 128, 512], P(None, 'gy', 'gx'), may hold values from 0.2 to 2
Outputs:
- pressure: float32 [16, 128, 512], P(None, 'gy', 'gx')
- coarse_residual: float32 [8, 64, 256], P(None, 'gy', 'gx')
- coarse_correction: float32 [8, 64, 256], P(None, 'gy')
All inputs are finite; a program needn't handle non-finite values.
Results may differ from a plain program's by a relative error of at most 0.0001.
Values sent between devices are 32-bit elements; how exact they have to be, the bound alone decides.
A program may use at most 128 MiB of HBM per device.

v0:
```python
import jax
import jax.numpy as jnp
from jax import lax
from jax.sharding import PartitionSpec as P

COARSE = 3
RELAX = 0.8


def extended(value, sides, width):
    for axis, dim in sides:
        peers, length = (lax.axis_size(axis), value.shape[dim])
        up = [(i, (i + 1) % peers) for i in range(peers - 1)]
        down = [(j, i) for i, j in up]
        last = lax.slice_in_dim(value, length - width, length, axis=dim)
        leading = lax.slice_in_dim(value, 0, width, axis=dim)
        before = lax.ppermute(last, axis, up)
        after = lax.ppermute(leading, axis, down)
        value = jnp.concatenate([before, value, after], axis=dim)
    return value


def from_behind(value, axis, steps):
    count = lax.axis_size(axis)
    leading, last = (max(0, -steps), min(count, count - steps))
    return lax.ppermute(value, axis, [(source, source + steps) for source in range(leading, last)])


def shifted(values, offset, axis_dim, filler):
    length = values.shape[axis_dim]
    if offset > 0:
        border = jnp.full_like(lax.slice_in_dim(values, 0, offset, axis=axis_dim), filler)
        return jnp.concatenate(
            [border, lax.slice_in_dim(values, 0, length - offset, axis=axis_dim)], axis=axis_dim
        )
    amount = -offset
    border = jnp.full_like(lax.slice_in_dim(values, 0, amount, axis=axis_dim), filler)
    return jnp.concatenate(
        [lax.slice_in_dim(values, amount, length, axis=axis_dim), border], axis=axis_dim
    )


def line_solve(low_band, diagonal, up_band, right_side, axis_dim):
    length = right_side.shape[axis_dim]
    stride = 1
    while stride < length:
        before = shifted(diagonal, stride, axis_dim, 1.0)
        after = shifted(diagonal, -stride, axis_dim, 1.0)
        weight_low = -low_band / before
        weight_up = -up_band / after
        new_diag = (
            diagonal
            + weight_low * shifted(up_band, stride, axis_dim, 0.0)
            + weight_up * shifted(low_band, -stride, axis_dim, 0.0)
        )
        new_right = (
            right_side
            + weight_low * shifted(right_side, stride, axis_dim, 0.0)
            + weight_up * shifted(right_side, -stride, axis_dim, 0.0)
        )
        low_band = weight_low * shifted(low_band, stride, axis_dim, 0.0)
        up_band = weight_up * shifted(up_band, -stride, axis_dim, 0.0)
        diagonal = new_diag
        right_side = new_right
        stride = stride * 2
    return right_side / diagonal


def top_masked(coupling):
    levels = coupling.shape[0]
    keep = (jnp.arange(levels) < levels - 1)[:, None, None]
    return jnp.where(keep, coupling, jnp.zeros_like(coupling))


def vertical(field, z_low, z_top):
    return z_low * shifted(field, 1, 0, 0.0) + z_top * shifted(field, -1, 0, 0.0)


def restrict(field):
    levels, rows, columns = field.shape
    blocks = field.reshape(levels // 2, 2, rows // 2, 2, columns // 2, 2)
    return jnp.sum(blocks, axis=(1, 3, 5)) * 0.125


def y_rim(field):
    return extended(field, (("gy", 1),), 1)


def x_return(solved):
    return lax.all_to_all(solved, "gx", split_axis=2, concat_axis=0, tiled=True)


def y_return(solved):
    return lax.all_to_all(solved, "gy", split_axis=1, concat_axis=0, tiled=True)


def x_solve(diag_lines, band_lines, source_lines):
    return line_solve(-shifted(band_lines, 1, 2, 0.0), diag_lines, -band_lines, source_lines, 2)


def y_solve(diag_lines, band_lines, source_lines):
    return line_solve(-shifted(band_lines, 1, 1, 0.0), diag_lines, -band_lines, source_lines, 1)


def body(forcing, pressure_in, x_coupling, y_coupling, z_coupling, damping):
    z_top = top_masked(z_coupling)
    z_low = shifted(z_top, 1, 0, 0.0)
    x_left = jnp.concatenate(
        [from_behind(x_coupling[:, :, -1:], "gx", 1), x_coupling[:, :, :-1]], axis=2
    )
    y_left = jnp.concatenate(
        [from_behind(y_coupling[:, -1:, :], "gy", 1), y_coupling[:, :-1, :]], axis=1
    )
    diagonal = x_left + x_coupling + y_left + y_coupling + z_low + z_top + damping
    field = pressure_in
    for repeat in range(2):
        padded = y_rim(field)
        source = (
            forcing
            + y_left * padded[:, :-2, :]
            + y_coupling * padded[:, 2:, :]
            + vertical(field, z_low, z_top)
        )
        source_lines, diag_lines, band_lines = (
            lax.all_to_all(source, "gx", split_axis=0, concat_axis=2, tiled=True),
            lax.all_to_all(diagonal, "gx", split_axis=0, concat_axis=2, tiled=True),
            lax.all_to_all(x_coupling, "gx", split_axis=0, concat_axis=2, tiled=True),
        )
        field = x_return(x_solve(diag_lines, band_lines, source_lines))
        padded = extended(field, (("gx", 2),), 1)
        source = (
            forcing
            + x_left * padded[:, :, :-2]
            + x_coupling * padded[:, :, 2:]
            + vertical(field, z_low, z_top)
        )
        source_lines, diag_lines, band_lines = (
            lax.all_to_all(source, "gy", split_axis=0, concat_axis=1, tiled=True),
            lax.all_to_all(diagonal, "gy", split_axis=0, concat_axis=1, tiled=True),
            lax.all_to_all(y_coupling, "gy", split_axis=0, concat_axis=1, tiled=True),
        )
        field = y_return(y_solve(diag_lines, band_lines, source_lines))
    padded = extended(field, (("gy", 1), ("gx", 2)), 1)
    applied = (
        diagonal * field
        - x_left * padded[:, 1:-1, :-2]
        - x_coupling * padded[:, 1:-1, 2:]
        - y_left * padded[:, :-2, 1:-1]
        - y_coupling * padded[:, 2:, 1:-1]
        - vertical(field, z_low, z_top)
    )
    coarse_residual = restrict(forcing - applied)
    coarse_x = restrict(x_coupling)
    coarse_y = restrict(y_coupling)
    coarse_z = restrict(z_coupling)
    coarse_damp = restrict(damping)
    whole_res, whole_x, whole_y, whole_z, whole_damp = (
        lax.all_gather(coarse_residual, "gx", axis=2, tiled=True),
        lax.all_gather(coarse_x, "gx", axis=2, tiled=True),
        lax.all_gather(coarse_y, "gx", axis=2, tiled=True),
        lax.all_gather(coarse_z, "gx", axis=2, tiled=True),
        lax.all_gather(coarse_damp, "gx", axis=2, tiled=True),
    )
    cz_top = top_masked(whole_z)
    cz_low = shifted(cz_top, 1, 0, 0.0)
    cx_left = shifted(whole_x, 1, 2, 0.0)
    cy_left = jnp.concatenate(
        [from_behind(whole_y[:, -1:, :], "gy", 1), whole_y[:, :-1, :]], axis=1
    )
    coarse_diag = cx_left + whole_x + cy_left + whole_y + cz_low + cz_top + whole_damp
    correction = RELAX * whole_res / coarse_diag
    for repeat in range(COARSE - 1):
        padded = extended(correction, (("gy", 1),), 1)
        applied_coarse = (
            coarse_diag * correction
            - cx_left * shifted(correction, 1, 2, 0.0)
            - whole_x * shifted(correction, -1, 2, 0.0)
            - cy_left * padded[:, :-2, :]
            - whole_y * padded[:, 2:, :]
            - vertical(correction, cz_low, cz_top)
        )
        correction = correction + RELAX * (whole_res - applied_coarse) / coarse_diag
    return (field, coarse_residual, correction)


def solution(mesh):
    in_specs = (
        P(None, "gy", "gx"),
        P(None, "gy", "gx"),
        P(None, "gy", "gx"),
        P(None, "gy", "gx"),
        P(None, "gy", "gx"),
        P(None, "gy", "gx"),
    )
    out_specs = (P(None, "gy", "gx"), P(None, "gy", "gx"), P(None, "gy", None))
    return jax.shard_map(body, mesh=mesh, in_specs=in_specs, out_specs=out_specs, check_vma=False)
```

profile of v0, /device:TPU:4, one launch (start us, length us, event | category | flops | bytes accessed | tf_op | source)
XLA Modules:
  0.0 384.3 jit_solution(15006799556907630283)
XLA Ops:
  0.6 4.9 %all-to-all-start.1 = ((f32[16,16,128]{2,1,0:T(8,128)}), f32[16,16,128]{2,1,0:T(8,128)S(1)}, u32[]{:S(2)}, u32[]{:S(2)}) async-start(f32[16,16,128]{2,1,0:T(8,128)} %param.8), calls=%async_computation.1 | async-start | bytes 262144 | tf_op jit(solution)/shard_map/all_to_all | solution.py:127
  6.4 1.9 collective-permute-start.2
  8.3 4.5 %collective-permute-start.3 = (f32[16,1,128]{2,1,0:T(1,128)S(1)}, f32[16,1,128]{2,1,0:T(1,128)S(1)}, u32[]{:S(2)}, u32[]{:S(2)}) collective-permute-start(f32[16,1,128]{2,1,0:T(1,128)S(1)} %get-tuple-element.266), channel_id=1, source_target_pairs={{1,0},{2,1},{3,2},{4,3},{5,4},{6,5},{7,6},{9,8},{10,9},{11,10},{12... | collective-permute-start | bytes 24584 | tf_op jit(solution)/shard_map/ppermute | solution.py:18
  13.7 1.9 collective-permute-start.1
  16.6 3.9 %collective-permute-start = (f32[16,16,1]{2,1,0:T(8,128)S(1)}, f32[16,16,1]{2,1,0:T(8,128)S(1)}, u32[]{:S(2)}, u32[]{:S(2)}) collective-permute-start(f32[16,16,1]{2,1,0:T(8,128)S(1)} %slice.761), channel_id=1, source_target_pairs={{0,8},{8,16},{16,24},{1,9},{9,17},{17,25},{2,10},{10,18},{18,26},{... | collective-permute-start | bytes 3080 | tf_op jit(solution)/shard_map/ppermute | solution.py:26
  22.6 1.6 collective-permute-done
  24.2 2.2 add_add_fusion
  26.4 11.4 %all_to_all.236 = f32[16,16,128]{2,1,0:T(8,128)S(1)} all-to-all(f32[16,16,128]{2,1,0:T(8,128)S(1)} %get-tuple-element.78), channel_id=1, replica_groups=mesh['gx'=4,'gy'=8] {'gx'}, dimensions={0} | all-to-all | bytes 262144 | tf_op jit(solution)/shard_map/all_to_all | solution.py:125
  37.8 3.3 all-to-all-start.2
  41.4 5.6 %all-to-all-done.2 = f32[16,16,128]{2,1,0:T(8,128)S(1)} async-done(((f32[16,16,128]{2,1,0:T(8,128)}), f32[16,16,128]{2,1,0:T(8,128)S(1)}, u32[]{:S(2)}, u32[]{:S(2)}) %all-to-all-start.2) | async-done | bytes 131104 | tf_op jit(solution)/shard_map/all_to_all | solution.py:126
  47.0 3.3 all-to-all-start.5
  56.7 4.2 %all-to-all-start.6 = ((f32[16,16,128]{2,1,0:T(8,128)}), f32[16,16,128]{2,1,0:T(8,128)S(1)}, u32[]{:S(2)}, u32[]{:S(2)}) async-start(f32[16,16,128]{2,1,0:T(8,128)} %get-tuple-element.76), calls=%async_computation.6 | async-start | bytes 262144 | tf_op jit(solution)/shard_map/all_to_all | solution.py:139
  61.4 1.5 reshape.34
  62.8 2.1 all-to-all-done.6
  64.9 3.3 all-to-all-start.3
  68.3 9.7 %reshape.31 = f32[8,2,8,2,64,2]{5,4,3,2,1,0:T(8,128)} reshape(f32[16,16,128]{2,1,0:T(8,128)S(1)} %copy-done) | data formatting | bytes 262144 | tf_op jit(solution)/shard_map/reshape | solution.py:81
  78.0 4.7 %reduce_sum.47 = f32[8,8,64]{2,1,0:T(8,128)} reduce(f32[8,2,8,2,64,2]{5,4,3,2,1,0:T(8,128)} %reshape.31, f32[]{:T(128)} %constant.7.clone.1), dimensions={1,3,5}, to_apply=%region_2.3 | reduce | flops 28672 | bytes 147460 | tf_op jit(solution)/shard_map/reduce_sum | solution.py:82
  85.4 3.9 %collective-permute-start.4 = (f32[16,16,1]{2,1,0:T(8,128)S(1)}, f32[16,16,1]{2,1,0:T(8,128)S(1)}, u32[]{:S(2)}, u32[]{:S(2)}) collective-permute-start(f32[16,16,1]{2,1,0:T(8,128)S(1)} %get-tuple-element.186), channel_id=1, source_target_pairs={{0,8},{8,16},{16,24},{1,9},{9,17},{17,25},{2,10},{10,18},{18,26},{... | collective-permute-start | bytes 3080 | tf_op jit(solution)/shard_map/ppermute | solution.py:17
  89.2 1.3 collective-permute-start.5
  91.7 4.4 %collective-permute-done.5 = f32[16,16,1]{2,1,0:T(8,128)S(1)} collective-permute-done((f32[16,16,1]{2,1,0:T(8,128)S(1)}, f32[16,16,1]{2,1,0:T(8,128)S(1)}, u32[]{:S(2)}, u32[]{:S(2)}) %collective-permute-start.5) | collective-permute-done | bytes 1056 | tf_op jit(solution)/shard_map/ppermute | solution.py:18
  97.0 4.8 %all-to-all-start.4 = ((f32[16,16,128]{2,1,0:T(8,128)}), f32[16,16,128]{2,1,0:T(8,128)S(1)}, u32[]{:S(2)}, u32[]{:S(2)}) async-start(f32[16,16,128]{2,1,0:T(8,128)} %fusion.22), calls=%async_computation.4 | async-start | bytes 262144 | tf_op jit(solution)/shard_map/all_to_all | solution.py:138
  101.8 4.0 %all-to-all-done.4 = f32[16,16,128]{2,1,0:T(8,128)S(1)} async-done(((f32[16,16,128]{2,1,0:T(8,128)}), f32[16,16,128]{2,1,0:T(8,128)S(1)}, u32[]{:S(2)}, u32[]{:S(2)}) %all-to-all-start.4) | async-done | bytes 131104 | tf_op jit(solution)/shard_map/all_to_all | solution.py:138
  109.7 5.6 %all-to-all-start.7 = ((f32[2,128,128]{2,0,1:T(2,128)}), f32[2,128,128]{2,0,1:T(2,128)}, u32[]{:S(2)}, u32[]{:S(2)}) async-start(f32[2,128,128]{2,0,1:T(2,128)} %copy.192), calls=%async_computation.7 | async-start | bytes 262144 | tf_op jit(solution)/shard_map/all_to_all | solution.py:94
  115.5 21.7 %all_gather.17 = f32[8,8,256]{1,0,2:T(8,128)S(1)} all-gather(f32[8,8,64]{1,0,2:T(8,128)S(1)} %copy.208), channel_id=1, replica_groups=mesh['gx'=4,'gy'=8] {'gx'}, dimensions={2}, use_global_device_ids=true | all-gather | bytes 81920 | tf_op jit(solution)/shard_map/all_gather | solution.py:160
  137.9 2.1 collective-permute-start.14
  139.9 9.7 %reshape.32 = f32[8,2,8,2,64,2]{5,4,3,2,1,0:T(8,128)} reshape(f32[16,16,128]{2,1,0:T(8,128)S(1)} %copy-done.2) | data formatting | bytes 262144 | tf_op jit(solution)/shard_map/reshape | solution.py:81
  149.7 4.0 %reduce_sum.48 = f32[8,8,64]{2,1,0:T(8,128)S(1)} reduce(f32[8,2,8,2,64,2]{5,4,3,2,1,0:T(8,128)} %reshape.32, f32[]{:T(128)} %constant.7.clone.1), dimensions={1,3,5}, to_apply=%region_3.4 | reduce | flops 28672 | bytes 147460 | tf_op jit(solution)/shard_map/reduce_sum | solution.py:82
  154.6 3.5 collective-permute-start.6
  158.1 3.0 collective-permute-start.7
  161.2 1.3 collective-permute-done.7
  163.2 3.9 %all-to-all-start.8 = ((f32[16,16,128]{2,1,0:T(8,128)}), f32[16,16,128]{2,1,0:T(8,128)}, u32[]{:S(2)}, u32[]{:S(2)}) async-start(f32[16,16,128]{2,1,0:T(8,128)} %fusion.17), calls=%async_computation.8 | async-start | bytes 262144 | tf_op jit(solution)/shard_map/all_to_all | solution.py:125
  167.2 9.7 %reshape.33 = f32[8,2,8,2,64,2]{5,4,3,2,1,0:T(8,128)} reshape(f32[16,16,128]{2,1,0:T(8,128)S(1)} %copy-done.51) | data formatting | bytes 262144 | tf_op jit(solution)/shard_map/reshape | solution.py:81
  176.9 9.7 %reshape.30 = f32[8,2,8,2,64,2]{5,4,3,2,1,0:T(8,128)} reshape(f32[16,16,128]{2,1,0:T(8,128)S(1)} %copy-done.1) | data formatting | bytes 262144 | tf_op jit(solution)/shard_map/reshape | solution.py:81
  186.6 4.6 %reduce_sum.49 = f32[8,8,64]{2,1,0:T(8,128)} reduce(f32[8,2,8,2,64,2]{5,4,3,2,1,0:T(8,128)} %reshape.33, f32[]{:T(128)} %constant.7.clone.1), dimensions={1,3,5}, to_apply=%region_4.5 | reduce | flops 28672 | bytes 147460 | tf_op jit(solution)/shard_map/reduce_sum | solution.py:82
  192.0 23.2 %all_gather.18 = f32[8,8,256]{1,0,2:T(8,128)S(1)} all-gather(f32[8,8,64]{1,0,2:T(8,128)} %copy.213), channel_id=1, replica_groups=mesh['gx'=4,'gy'=8] {'gx'}, dimensions={2}, use_global_device_ids=true | all-gather | bytes 81920 | tf_op jit(solution)/shard_map/all_gather | solution.py:161
  216.2 4.7 %reduce_sum.46 = f32[8,8,64]{2,1,0:T(8,128)} reduce(f32[8,2,8,2,64,2]{5,4,3,2,1,0:T(8,128)} %reshape.30, f32[]{:T(128)} %constant.7.clone.1), dimensions={1,3,5}, to_apply=%region_1.2 | reduce | flops 28672 | bytes 147460 | tf_op jit(solution)/shard_map/reduce_sum | solution.py:82
  225.3 1.5 reshape.36
  226.7 4.3 %all-to-all-start.9 = ((f32[4,1,8192]{2,1,0:T(1,128)}), f32[4,1,8192]{2,1,0:T(1,128)S(1)}, u32[]{:S(2)}, u32[]{:S(2)}) async-start(f32[4,1,8192]{2,1,0:T(1,128)} %reshape.36), calls=%async_computation.9 | async-start | bytes 262144 | tf_op jit(solution)/shard_map/all_to_all | solution.py:90
  231.0 1.5 broadcast_select_fusion.1
  232.6 4.4 %all-to-all-done.9 = f32[4,1,8192]{2,1,0:T(1,128)S(1)} async-done(((f32[4,1,8192]{2,1,0:T(1,128)}), f32[4,1,8192]{2,1,0:T(1,128)S(1)}, u32[]{:S(2)}, u32[]{:S(2)}) %all-to-all-start.9) | async-done | bytes 131104 | tf_op jit(solution)/shard_map/all_to_all | solution.py:90
  239.1 3.3 collective-permute-start.8
  244.9 4.4 %collective-permute-done.9 = f32[16,16,1]{2,1,0:T(8,128)S(1)} collective-permute-done((f32[16,16,1]{2,1,0:T(8,128)S(1)}, f32[16,16,1]{2,1,0:T(8,128)S(1)}, u32[]{:S(2)}, u32[]{:S(2)}) %collective-permute-start.9) | collective-permute-done | bytes 1056 | tf_op jit(solution)/shard_map/ppermute | solution.py:18
  249.2 1.8 fusion.12
  251.0 3.5 all-to-all-start.10
  254.6 1.4 broadcast_multiply_fusion
  255.9 2.4 all-to-all-done.10
  263.4 4.8 %all-to-all-start.11 = ((f32[2,128,128]{2,0,1:T(2,128)}), f32[2,128,128]{2,0,1:T(2,128)S(1)}, u32[]{:S(2)}, u32[]{:S(2)}) async-start(f32[2,128,128]{2,0,1:T(2,128)} %copy.200), calls=%async_computation.11 | async-start | bytes 262144 | tf_op jit(solution)/shard_map/all_to_all | solution.py:94
  270.0 21.7 %all_gather.19 = f32[8,8,256]{1,0,2:T(8,128)S(1)} all-gather(f32[8,8,64]{1,0,2:T(8,128)S(1)} %copy.215), channel_id=1, replica_groups=mesh['gx'=4,'gy'=8] {'gx'}, dimensions={2}, use_global_device_ids=true | all-gather | bytes 81920 | tf_op jit(solution)/shard_map/all_gather | solution.py:162
  291.8 1.9 collective-permute-start.10
  293.7 4.5 %collective-permute-start.11 = (f32[16,1,128]{2,1,0:T(1,128)S(1)}, f32[16,1,128]{2,1,0:T(1,128)S(1)}, u32[]{:S(2)}, u32[]{:S(2)}) collective-permute-start(f32[16,1,128]{2,1,0:T(1,128)S(1)} %get-tuple-element.84), channel_id=1, source_target_pairs={{1,0},{2,1},{3,2},{4,3},{5,4},{6,5},{7,6},{9,8},{10,9},{11,10},{12... | collective-permute-start | bytes 24584 | tf_op jit(solution)/shard_map/ppermute | solution.py:18
  298.2 20.6 %all_gather.16 = f32[8,8,256]{1,0,2:T(8,128)} all-gather(f32[8,8,64]{1,0,2:T(8,128)S(1)} %copy.205), channel_id=1, replica_groups=mesh['gx'=4,'gy'=8] {'gx'}, dimensions={2}, use_global_device_ids=true | all-gather | bytes 81920 | tf_op jit(solution)/shard_map/all_gather | solution.py:159
  320.4 1.5 copy.206
  322.8 2.3 collective-permute-start.12
  326.5 1.8 collective-permute-done.12
  328.3 4.4 %collective-permute-done.13 = f32[16,18,1]{2,1,0:T(8,128)S(1)} collective-permute-done((f32[16,18,1]{2,1,0:T(8,128)S(1)}, f32[16,18,1]{2,1,0:T(8,128)S(1)}, u32[]{:S(2)}, u32[]{:S(2)}) %collective-permute-start.13) | collective-permute-done | bytes 1184 | tf_op jit(solution)/shard_map/ppermute | solution.py:18
  333.9 9.7 %reshape.29 = f32[8,2,8,2,64,2]{5,4,3,2,1,0:T(8,128)} reshape(f32[16,16,128]{2,1,0:T(8,128)S(1)} %fusion.3) | data formatting | bytes 262144 | tf_op jit(solution)/shard_map/reshape | solution.py:81
  343.6 4.0 %reduce_sum.45 = f32[8,8,64]{2,1,0:T(8,128)S(1)} reduce(f32[8,2,8,2,64,2]{5,4,3,2,1,0:T(8,128)} %reshape.29, f32[]{:T(128)} %constant.7.clone.1), dimensions={1,3,5}, to_apply=%region_0.1 | reduce | flops 28672 | bytes 147460 | tf_op jit(solution)/shard_map/reduce_sum | solution.py:82
  347.8 19.2 %all_gather.15 = f32[8,8,256]{1,0,2:T(8,128)S(1)} all-gather(f32[8,8,64]{1,0,2:T(8,128)S(1)} %copy.203), channel_id=1, replica_groups=mesh['gx'=4,'gy'=8] {'gx'}, dimensions={2}, use_global_device_ids=true | all-gather | bytes 81920 | tf_op jit(solution)/shard_map/all_gather | solution.py:158
  367.6 1.9 collective-permute-start.16
  369.6 2.4 collective-permute-start.15
  372.0 3.4 collective-permute-done.15
  375.7 1.9 collective-permute-start.18
  377.6 2.4 collective-permute-start.17
  380.1 3.4 collective-permute-done.17
  (390 shorter events, 45.9 us)
Async XLA Ops:
  0.6 25.7 %all-to-all-start.1 = ((f32[16,16,128]{2,1,0:T(8,128)}), f32[16,16,128]{2,1,0:T(8,128)S(1)}, u32[]{:S(2)}, u32[]{:S(2)}) async-start(f32[16,16,128]{2,1,0:T(8,128)} %param.8), calls=%async_computation.1 | async-start | bytes 262144 | tf_op jit(solution)/shard_map/all_to_all | solution.py:127
  6.4 17.8 %collective-permute-start.2 = (f32[16,1,128]{2,1,0:T(1,128)S(1)}, f32[16,1,128]{2,1,0:T(1,128)S(1)}, u32[]{:S(2)}, u32[]{:S(2)}) collective-permute-start(f32[16,1,128]{2,1,0:T(1,128)S(1)} %get-tuple-element.265), channel_id=1, source_target_pairs={{0,1},{1,2},{2,3},{3,4},{4,5},{5,6},{6,7},{8,9},{9,10},{10,11},{11... | collective-permute-start | bytes 24584 | tf_op jit(solution)/shard_map/ppermute | solution.py:17
  8.3 15.9 %collective-permute-start.3 = (f32[16,1,128]{2,1,0:T(1,128)S(1)}, f32[16,1,128]{2,1,0:T(1,128)S(1)}, u32[]{:S(2)}, u32[]{:S(2)}) collective-permute-start(f32[16,1,128]{2,1,0:T(1,128)S(1)} %get-tuple-element.266), channel_id=1, source_target_pairs={{1,0},{2,1},{3,2},{4,3},{5,4},{6,5},{7,6},{9,8},{10,9},{11,10},{12... | collective-permute-start | bytes 24584 | tf_op jit(solution)/shard_map/ppermute | solution.py:18
  13.7 10.5 %collective-permute-start.1 = (f32[16,1,128]{2,1,0:T(1,128)S(1)}, f32[16,1,128]{2,1,0:T(1,128)S(1)}, u32[]{:S(2)}, u32[]{:S(2)}) collective-permute-start(f32[16,1,128]{2,1,0:T(1,128)S(1)} %slice.763), channel_id=1, source_target_pairs={{0,1},{1,2},{2,3},{3,4},{4,5},{5,6},{6,7},{8,9},{9,10},{10,11},{11... | collective-permute-start | bytes 24584 | tf_op jit(solution)/shard_map/ppermute | solution.py:26
  16.6 7.5 %collective-permute-start = (f32[16,16,1]{2,1,0:T(8,128)S(1)}, f32[16,16,1]{2,1,0:T(8,128)S(1)}, u32[]{:S(2)}, u32[]{:S(2)}) collective-permute-start(f32[16,16,1]{2,1,0:T(8,128)S(1)} %slice.761), channel_id=1, source_target_pairs={{0,8},{8,16},{16,24},{1,9},{9,17},{17,25},{2,10},{10,18},{18,26},{... | collective-permute-start | bytes 3080 | tf_op jit(solution)/shard_map/ppermute | solution.py:26
  26.4 69.7 %copy-start.15 = (f32[16,16,128]{2,1,0:T(8,128)}, f32[16,16,128]{2,1,0:T(8,128)S(1)}, u32[]{:S(2)}) copy-start(f32[16,16,128]{2,1,0:T(8,128)S(1)} %get-tuple-element.77) | copy-start | bytes 393220
  37.8 9.2 %all-to-all-start.2 = ((f32[16,16,128]{2,1,0:T(8,128)}), f32[16,16,128]{2,1,0:T(8,128)S(1)}, u32[]{:S(2)}, u32[]{:S(2)}) async-start(f32[16,16,128]{2,1,0:T(8,128)} %get-tuple-element.76), calls=%async_computation.2 | async-start | bytes 262144 | tf_op jit(solution)/shard_map/all_to_all | solution.py:126
  47.0 9.6 %all-to-all-start.5 = ((f32[16,16,128]{2,1,0:T(8,128)}), f32[16,16,128]{2,1,0:T(8,128)S(1)}, u32[]{:S(2)}, u32[]{:S(2)}) async-start(f32[16,16,128]{2,1,0:T(8,128)} %param.9), calls=%async_computation.5 | async-start | bytes 262144 | tf_op jit(solution)/shard_map/all_to_all | solution.py:140
  54.5 13.7 %copy-start.21 = (f32[4,16,512]{2,1,0:T(8,128)}, f32[4,16,512]{2,1,0:T(8,128)S(1)}, u32[]{:S(2)}) copy-start(f32[4,16,512]{2,1,0:T(8,128)S(1)} %get-tuple-element.51) | copy-start | bytes 393220
  54.5 13.8 %copy-start = (f32[16,16,128]{2,1,0:T(8,128)S(1)}, f32[16,16,128]{2,1,0:T(8,128)}, u32[]{:S(2)}) copy-start(f32[16,16,128]{2,1,0:T(8,128)} %param.9) | copy-start | bytes 393220
  55.2 13.0 %copy-start.31 = (f32[4,16,512]{2,1,0:T(8,128)}, f32[4,16,512]{2,1,0:T(8,128)S(1)}, u32[]{:S(2)}) copy-start(f32[4,16,512]{2,1,0:T(8,128)S(1)} %get-tuple-element.44) | copy-start | bytes 393220
  55.5 12.8 %copy-start.55 = (f32[4,16,512]{2,1,0:T(8,128)}, f32[4,16,512]{2,1,0:T(8,128)S(1)}, u32[]{:S(2)}) copy-start(f32[4,16,512]{2,1,0:T(8,128)S(1)} %get-tuple-element.46) | copy-start | bytes 393220
  55.8 26.9 %copy-start.34 = (f32[4,16,512]{2,1,0:T(8,128)}, f32[4,16,512]{2,1,0:T(8,128)S(1)}, u32[]{:S(2)}) copy-start(f32[4,16,512]{2,1,0:T(8,128)S(1)} %get-tuple-element.40) | copy-start | bytes 393220
  55.8 26.9 %copy-start.43 = (f32[4,16,512]{2,1,0:T(8,128)}, f32[4,16,512]{2,1,0:T(8,128)S(1)}, u32[]{:S(2)}) copy-start(f32[4,16,512]{2,1,0:T(8,128)S(1)} %get-tuple-element.39) | copy-start | bytes 393220
  55.9 26.8 %copy-start.38 = (f32[4,16,512]{2,1,0:T(8,128)}, f32[4,16,512]{2,1,0:T(8,128)S(1)}, u32[]{:S(2)}) copy-start(f32[4,16,512]{2,1,0:T(8,128)S(1)} %get-tuple-element.41) | copy-start | bytes 393220
  56.6 26.1 %copy-start.47 = (f32[4,16,512]{2,1,0:T(8,128)}, f32[4,16,512]{2,1,0:T(8,128)S(1)}, u32[]{:S(2)}) copy-start(f32[4,16,512]{2,1,0:T(8,128)S(1)} %get-tuple-element.190) | copy-start | bytes 393220
  56.6 26.1 %copy-start.64 = (f32[4,16,256]{2,1,0:T(8,128)}, f32[4,16,256]{2,1,0:T(8,128)S(1)}, u32[]{:S(2)}) copy-start(f32[4,16,256]{2,1,0:T(8,128)S(1)} %slice.1048) | copy-start | bytes 196612
  56.7 8.2 %all-to-all-start.6 = ((f32[16,16,128]{2,1,0:T(8,128)}), f32[16,16,128]{2,1,0:T(8,128)S(1)}, u32[]{:S(2)}, u32[]{:S(2)}) async-start(f32[16,16,128]{2,1,0:T(8,128)} %get-tuple-element.76), calls=%async_computation.6 | async-start | bytes 262144 | tf_op jit(solution)/shard_map/all_to_all | solution.py:139
  64.9 17.9 %all-to-all-start.3 = ((f32[4,1,8192]{2,1,0:T(1,128)}), f32[4,1,8192]{2,1,0:T(1,128)S(1)}, u32[]{:S(2)}, u32[]{:S(2)}) async-start(f32[4,1,8192]{2,1,0:T(1,128)} %reshape.34), calls=%async_computation.3 | async-start | bytes 262144 | tf_op jit(solution)/shard_map/all_to_all | solution.py:90
  68.2 14.4 %copy-start.77 = (f32[16,16,128]{2,1,0:T(8,128)S(1)}, f32[16,16,128]{2,1,0:T(8,128)}, u32[]{:S(2)}) copy-start(f32[16,16,128]{2,1,0:T(8,128)} %copy-done.76) | copy-start | bytes 393220
  78.0 18.1 %copy-start.1 = (f32[16,16,128]{2,1,0:T(8,128)S(1)}, f32[16,16,128]{2,1,0:T(8,128)}, u32[]{:S(2)}) copy-start(f32[16,16,128]{2,1,0:T(8,128)} %param.8) | copy-start | bytes 393220
  78.0 18.1 %copy-start.2 = (f32[16,16,128]{2,1,0:T(8,128)S(1)}, f32[16,16,128]{2,1,0:T(8,128)}, u32[]{:S(2)}) copy-start(f32[16,16,128]{2,1,0:T(8,128)} %param.10) | copy-start | bytes 393220
  78.0 18.1 %copy-start.3 = (f32[16,16,128]{2,1,0:T(8,128)S(1)}, f32[16,16,128]{2,1,0:T(8,128)}, u32[]{:S(2)}) copy-start(f32[16,16,128]{2,1,0:T(8,128)} %param.6) | copy-start | bytes 393220
  85.4 6.4 %collective-permute-start.4 = (f32[16,16,1]{2,1,0:T(8,128)S(1)}, f32[16,16,1]{2,1,0:T(8,128)S(1)}, u32[]{:S(2)}, u32[]{:S(2)}) collective-permute-start(f32[16,16,1]{2,1,0:T(8,128)S(1)} %get-tuple-element.186), channel_id=1, source_target_pairs={{0,8},{8,16},{16,24},{1,9},{9,17},{17,25},{2,10},{10,18},{18,26},{... | collective-permute-start | bytes 3080 | tf_op jit(solution)/shard_map/ppermute | solution.py:17
  89.2 6.9 %collective-permute-start.5 = (f32[16,16,1]{2,1,0:T(8,128)S(1)}, f32[16,16,1]{2,1,0:T(8,128)S(1)}, u32[]{:S(2)}, u32[]{:S(2)}) collective-permute-start(f32[16,16,1]{2,1,0:T(8,128)S(1)} %get-tuple-element.187), channel_id=1, source_target_pairs={{8,0},{16,8},{24,16},{9,1},{17,9},{25,17},{10,2},{18,10},{26,18},{... | collective-permute-start | bytes 3080 | tf_op jit(solution)/shard_map/ppermute | solution.py:18
  97.0 8.8 %all-to-all-start.4 = ((f32[16,16,128]{2,1,0:T(8,128)}), f32[16,16,128]{2,1,0:T(8,128)S(1)}, u32[]{:S(2)}, u32[]{:S(2)}) async-start(f32[16,16,128]{2,1,0:T(8,128)} %fusion.22), calls=%async_computation.4 | async-start | bytes 262144 | tf_op jit(solution)/shard_map/all_to_all | solution.py:138
  107.2 42.5 %copy-start.23 = (f32[2,128,128]{2,1,0:T(8,128)}, f32[2,128,128]{2,1,0:T(8,128)S(1)}, u32[]{:S(2)}) copy-start(f32[2,128,128]{2,1,0:T(8,128)S(1)} %get-tuple-element.17) | copy-start | bytes 393220
  109.7 44.0 %all-to-all-start.7 = ((f32[2,128,128]{2,0,1:T(2,128)}), f32[2,128,128]{2,0,1:T(2,128)}, u32[]{:S(2)}, u32[]{:S(2)}) async-start(f32[2,128,128]{2,0,1:T(2,128)} %copy.192), calls=%async_computation.7 | async-start | bytes 262144 | tf_op jit(solution)/shard_map/all_to_all | solution.py:94
  137.9 29.3 %copy-start.51 = (f32[16,16,128]{2,1,0:T(8,128)S(1)}, f32[16,16,128]{2,1,0:T(8,128)}, u32[]{:S(2)}) copy-start(f32[16,16,128]{2,1,0:T(8,128)} %param.11) | copy-start | bytes 393220
  137.9 184.1 %collective-permute-start.14 = (f32[8,1,256]{2,0,1:T(8,128)S(1)}, f32[8,1,256]{2,0,1:T(8,128)}, u32[]{:S(2)}, u32[]{:S(2)}) collective-permute-start(f32[8,1,256]{2,0,1:T(8,128)S(1)} %copy.209), channel_id=1, source_target_pairs={{0,1},{1,2},{2,3},{3,4},{4,5},{5,6},{6,7},{8,9},{9,10},{10,11},{11... | collective-permute-start | bytes 24584 | tf_op jit(solution)/shard_map/ppermute | solution.py:26
  154.6 6.5 %collective-permute-start.6 = (f32[16,1,128]{2,1,0:T(1,128)S(1)}, f32[16,1,128]{2,1,0:T(1,128)S(1)}, u32[]{:S(2)}, u32[]{:S(2)}) collective-permute-start(f32[16,1,128]{2,1,0:T(1,128)S(1)} %get-tuple-element.123), channel_id=1, source_target_pairs={{0,1},{1,2},{2,3},{3,4},{4,5},{5,6},{6,7},{8,9},{9,10},{10,11},{11... | collective-permute-start | bytes 24584 | tf_op jit(solution)/shard_map/ppermute | solution.py:17
  158.1 4.3 %collective-permute-start.7 = (f32[16,1,128]{2,1,0:T(1,128)S(1)}, f32[16,1,128]{2,1,0:T(1,128)S(1)}, u32[]{:S(2)}, u32[]{:S(2)}) collective-permute-start(f32[16,1,128]{2,1,0:T(1,128)S(1)} %get-tuple-element.124), channel_id=1, source_target_pairs={{1,0},{2,1},{3,2},{4,3},{5,4},{6,5},{7,6},{9,8},{10,9},{11,10},{12... | collective-permute-start | bytes 24584 | tf_op jit(solution)/shard_map/ppermute | solution.py:18
  163.2 57.7 %all-to-all-start.8 = ((f32[16,16,128]{2,1,0:T(8,128)}), f32[16,16,128]{2,1,0:T(8,128)}, u32[]{:S(2)}, u32[]{:S(2)}) async-start(f32[16,16,128]{2,1,0:T(8,128)} %fusion.17), calls=%async_computation.8 | async-start | bytes 262144 | tf_op jit(solution)/shard_map/all_to_all | solution.py:125
  191.2 31.7 %copy-start.6 = (f32[4,16,512]{2,1,0:T(8,128)S(1)}, f32[4,16,512]{2,1,0:T(8,128)}, u32[]{:S(2)}) copy-start(f32[4,16,512]{2,1,0:T(8,128)} %copy-done.5) | copy-start | bytes 393220
  222.8 35.6 %copy-start.29 = (f32[2,128,128]{2,1,0:T(8,128)S(1)}, f32[2,128,128]{2,1,0:T(8,128)}, u32[]{:S(2)}) copy-start(f32[2,128,128]{2,1,0:T(8,128)} %copy-done.28) | copy-start | bytes 393220
  223.0 36.4 %copy-start.12 = (f32[2,128,128]{2,1,0:T(8,128)S(1)}, f32[2,128,128]{2,1,0:T(8,128)}, u32[]{:S(2)}) copy-start(f32[2,128,128]{2,1,0:T(8,128)} %copy-done.11) | copy-start | bytes 393220
  223.0 36.4 %copy-start.14 = (f32[2,128,128]{2,1,0:T(8,128)S(1)}, f32[2,128,128]{2,1,0:T(8,128)}, u32[]{:S(2)}) copy-start(f32[2,128,128]{2,1,0:T(8,128)} %copy-done.13) | copy-start | bytes 393220
  223.2 36.3 %copy-start.18 = (f32[2,128,128]{2,1,0:T(8,128)S(1)}, f32[2,128,128]{2,1,0:T(8,128)}, u32[]{:S(2)}) copy-start(f32[2,128,128]{2,1,0:T(8,128)} %copy-done.17) | copy-start | bytes 393220
  223.2 36.3 %copy-start.20 = (f32[2,128,128]{2,1,0:T(8,128)S(1)}, f32[2,128,128]{2,1,0:T(8,128)}, u32[]{:S(2)}) copy-start(f32[2,128,128]{2,1,0:T(8,128)} %copy-done.19) | copy-start | bytes 393220
  226.7 10.2 %all-to-all-start.9 = ((f32[4,1,8192]{2,1,0:T(1,128)}), f32[4,1,8192]{2,1,0:T(1,128)S(1)}, u32[]{:S(2)}, u32[]{:S(2)}) async-start(f32[4,1,8192]{2,1,0:T(1,128)} %reshape.36), calls=%async_computation.9 | async-start | bytes 262144 | tf_op jit(solution)/shard_map/all_to_all | solution.py:90
  238.9 21.7 %copy-start.54 = (f32[2,128,128]{2,1,0:T(8,128)S(1)}, f32[2,128,128]{2,1,0:T(8,128)}, u32[]{:S(2)}) copy-start(f32[2,128,128]{2,1,0:T(8,128)} %copy-done.53) | copy-start | bytes 393220
  238.9 22.7 %copy-start.37 = (f32[2,128,128]{2,1,0:T(8,128)S(1)}, f32[2,128,128]{2,1,0:T(8,128)}, u32[]{:S(2)}) copy-start(f32[2,128,128]{2,1,0:T(8,128)} %copy-done.36) | copy-start | bytes 393220
  238.9 22.7 %copy-start.61 = (f32[2,128,128]{2,1,0:T(8,128)S(1)}, f32[2,128,128]{2,1,0:T(8,128)}, u32[]{:S(2)}) copy-start(f32[2,128,128]{2,1,0:T(8,128)} %copy-done.60) | copy-start | bytes 393220
  238.9 22.8 %copy-start.41 = (f32[2,128,128]{2,1,0:T(8,128)S(1)}, f32[2,128,128]{2,1,0:T(8,128)}, u32[]{:S(2)}) copy-start(f32[2,128,128]{2,1,0:T(8,128)} %copy-done.40) | copy-start | bytes 393220
  238.9 22.8 %copy-start.46 = (f32[2,128,128]{2,1,0:T(8,128)S(1)}, f32[2,128,128]{2,1,0:T(8,128)}, u32[]{:S(2)}) copy-start(f32[2,128,128]{2,1,0:T(8,128)} %copy-done.45) | copy-start | bytes 393220
  238.9 22.8 %copy-start.50 = (f32[2,128,128]{2,1,0:T(8,128)S(1)}, f32[2,128,128]{2,1,0:T(8,128)}, u32[]{:S(2)}) copy-start(f32[2,128,128]{2,1,0:T(8,128)} %copy-done.49) | copy-start | bytes 393220
  239.0 22.8 %copy-start.67 = (f32[2,64,128]{2,1,0:T(8,128)S(1)}, f32[2,64,128]{2,1,0:T(8,128)}, u32[]{:S(2)}) copy-start(f32[2,64,128]{2,1,0:T(8,128)} %copy-done.66) | copy-start | bytes 196612
  239.0 22.8 %copy-start.69 = (f32[2,64,128]{2,1,0:T(8,128)S(1)}, f32[2,64,128]{2,1,0:T(8,128)}, u32[]{:S(2)}) copy-start(f32[2,64,128]{2,1,0:T(8,128)} %copy-done.68) | copy-start | bytes 196612
  239.1 5.8 %collective-permute-start.8 = (f32[16,16,1]{2,1,0:T(8,128)S(1)}, f32[16,16,1]{2,1,0:T(8,128)S(1)}, u32[]{:S(2)}, u32[]{:S(2)}) collective-permute-start(f32[16,16,1]{2,1,0:T(8,128)S(1)} %get-tuple-element.101), channel_id=1, source_target_pairs={{0,8},{8,16},{16,24},{1,9},{9,17},{17,25},{2,10},{10,18},{18,26},{... | collective-permute-start | bytes 3080 | tf_op jit(solution)/shard_map/ppermute | solution.py:17
  242.4 6.9 %collective-permute-start.9 = (f32[16,16,1]{2,1,0:T(8,128)S(1)}, f32[16,16,1]{2,1,0:T(8,128)S(1)}, u32[]{:S(2)}, u32[]{:S(2)}) collective-permute-start(f32[16,16,1]{2,1,0:T(8,128)S(1)} %get-tuple-element.102), channel_id=1, source_target_pairs={{8,0},{16,8},{24,16},{9,1},{17,9},{25,17},{10,2},{18,10},{26,18},{... | collective-permute-start | bytes 3080 | tf_op jit(solution)/shard_map/ppermute | solution.py:18
  251.0 7.3 %all-to-all-start.10 = ((f32[16,16,128]{2,1,0:T(8,128)}), f32[16,16,128]{2,1,0:T(8,128)S(1)}, u32[]{:S(2)}, u32[]{:S(2)}) async-start(f32[16,16,128]{2,1,0:T(8,128)} %fusion.12), calls=%async_computation.10 | async-start | bytes 262144 | tf_op jit(solution)/shard_map/all_to_all | solution.py:138
  259.3 73.4 %copy-start.16 = (f32[16,16,128]{2,1,0:T(8,128)S(1)}, f32[16,16,128]{2,1,0:T(8,128)}, u32[]{:S(2)}) copy-start(f32[16,16,128]{2,1,0:T(8,128)} %copy-done.15) | copy-start | bytes 393220
  263.4 28.3 %all-to-all-start.11 = ((f32[2,128,128]{2,0,1:T(2,128)}), f32[2,128,128]{2,0,1:T(2,128)S(1)}, u32[]{:S(2)}, u32[]{:S(2)}) async-start(f32[2,128,128]{2,0,1:T(2,128)} %copy.200), calls=%async_computation.11 | async-start | bytes 262144 | tf_op jit(solution)/shard_map/all_to_all | solution.py:94
  291.7 51.9 %copy-start.4 = (f32[8,2,16,128]{3,2,1,0:T(8,128)}, f32[8,2,16,128]{3,2,1,0:T(8,128)S(1)}, u32[]{:S(2)}) copy-start(f32[8,2,16,128]{3,2,1,0:T(8,128)S(1)} %copy.202) | copy-start | bytes 393220
  291.8 30.9 %collective-permute-start.10 = (f32[16,1,128]{2,1,0:T(1,128)S(1)}, f32[16,1,128]{2,1,0:T(1,128)S(1)}, u32[]{:S(2)}, u32[]{:S(2)}) collective-permute-start(f32[16,1,128]{2,1,0:T(1,128)S(1)} %get-tuple-element.83), channel_id=1, source_target_pairs={{0,1},{1,2},{2,3},{3,4},{4,5},{5,6},{6,7},{8,9},{9,10},{10,11},{11... | collective-permute-start | bytes 24584 | tf_op jit(solution)/shard_map/ppermute | solution.py:17
  293.7 29.0 %collective-permute-start.11 = (f32[16,1,128]{2,1,0:T(1,128)S(1)}, f32[16,1,128]{2,1,0:T(1,128)S(1)}, u32[]{:S(2)}, u32[]{:S(2)}) collective-permute-start(f32[16,1,128]{2,1,0:T(1,128)S(1)} %get-tuple-element.84), channel_id=1, source_target_pairs={{1,0},{2,1},{3,2},{4,3},{5,4},{6,5},{7,6},{9,8},{10,9},{11,10},{12... | collective-permute-start | bytes 24584 | tf_op jit(solution)/shard_map/ppermute | solution.py:18
  322.8 5.5 %collective-permute-start.12 = (f32[16,18,1]{2,1,0:T(8,128)S(1)}, f32[16,18,1]{2,1,0:T(8,128)S(1)}, u32[]{:S(2)}, u32[]{:S(2)}) collective-permute-start(f32[16,18,1]{2,1,0:T(8,128)S(1)} %get-tuple-element.79), channel_id=1, source_target_pairs={{0,8},{8,16},{16,24},{1,9},{9,17},{17,25},{2,10},{10,18},{18,26},{... | collective-permute-start | bytes 3464 | tf_op jit(solution)/shard_map/ppermute | solution.py:17
  325.1 7.6 %collective-permute-start.13 = (f32[16,18,1]{2,1,0:T(8,128)S(1)}, f32[16,18,1]{2,1,0:T(8,128)S(1)}, u32[]{:S(2)}, u32[]{:S(2)}) collective-permute-start(f32[16,18,1]{2,1,0:T(8,128)S(1)} %get-tuple-element.80), channel_id=1, source_target_pairs={{8,0},{16,8},{24,16},{9,1},{17,9},{25,17},{10,2},{18,10},{26,18},{... | collective-permute-start | bytes 3464 | tf_op jit(solution)/shard_map/ppermute | solution.py:18
  333.9 33.5 %copy-start.42 = (f32[8,8,256]{2,1,0:T(8,128)S(1)}, f32[8,8,256]{2,1,0:T(8,128)}, u32[]{:S(2)}) copy-start(f32[8,8,256]{2,1,0:T(8,128)} %copy.214) | copy-start | bytes 196612
  347.6 36.6 %copy-start.79 = (f32[8,8,64]{2,1,0:T(8,128)}, f32[8,8,64]{2,1,0:T(8,128)S(1)}, u32[]{:S(2)}) copy-start(f32[8,8,64]{2,1,0:T(8,128)S(1)} %broadcast_multiply_fusion.4) | copy-start | bytes 49156
  367.6 4.4 %collective-permute-start.16 = (f32[8,1,256]{2,0,1:T(8,128)S(1)}, f32[8,1,256]{2,0,1:T(8,128)S(1)}, u32[]{:S(2)}, u32[]{:S(2)}) collective-permute-start(f32[8,1,256]{2,0,1:T(8,128)S(1)} %copy.220), channel_id=1, source_target_pairs={{1,0},{2,1},{3,2},{4,3},{5,4},{6,5},{7,6},{9,8},{10,9},{11,10},{12... | collective-permute-start | bytes 24584 | tf_op jit(solution)/shard_map/ppermute | solution.py:18
  369.6 5.9 %collective-permute-start.15 = (f32[8,1,256]{2,0,1:T(8,128)S(1)}, f32[8,1,256]{2,0,1:T(8,128)S(1)}, u32[]{:S(2)}, u32[]{:S(2)}) collective-permute-start(f32[8,1,256]{2,0,1:T(8,128)S(1)} %copy.218), channel_id=1, source_target_pairs={{0,1},{1,2},{2,3},{3,4},{4,5},{5,6},{6,7},{8,9},{9,10},{10,11},{11... | collective-permute-start | bytes 24584 | tf_op jit(solution)/shard_map/ppermute | solution.py:17
  375.7 4.4 %collective-permute-start.18 = (f32[8,1,256]{2,0,1:T(8,128)S(1)}, f32[8,1,256]{2,0,1:T(8,128)S(1)}, u32[]{:S(2)}, u32[]{:S(2)}) collective-permute-start(f32[8,1,256]{2,0,1:T(8,128)S(1)} %copy.227), channel_id=1, source_target_pairs={{1,0},{2,1},{3,2},{4,3},{5,4},{6,5},{7,6},{9,8},{10,9},{11,10},{12... | collective-permute-start | bytes 24584 | tf_op jit(solution)/shard_map/ppermute | solution.py:18
  377.6 5.9 %collective-permute-start.17 = (f32[8,1,256]{2,0,1:T(8,128)S(1)}, f32[8,1,256]{2,0,1:T(8,128)S(1)}, u32[]{:S(2)}, u32[]{:S(2)}) collective-permute-start(f32[8,1,256]{2,0,1:T(8,128)S(1)} %copy.225), channel_id=1, source_target_pairs={{0,1},{1,2},{2,3},{3,4},{4,5},{5,6},{6,7},{8,9},{9,10},{10,11},{11... | collective-permute-start | bytes 24584 | tf_op jit(solution)/shard_map/ppermute | solution.py:17
  (46 other events, 161.6 us)
where the time goes:
time: 387 us; the launch traced here: 384 us
  blocking collectives  118 us (30%)
  starting transfers between devices  95.2 us (25%)
  local copies, waits for them, and re-layouts  77.1 us (20%)
  other arithmetic  45.6 us (12%)
  waiting for transfers between devices  45.5 us (12%)
    reshape x5, local copies, waits for them, and re-layouts, restrict(): blocks = field.reshape(levels // 2, 2, rows // 2, 2, columns // 2, 2)  48.6 us
    all_gather x1, blocking collectives, body(): lax.all_gather(coarse_z, 'gx', axis=2, tiled=True)  23.2 us
    reduce_sum x5, other arithmetic, restrict(): return jnp.sum(blocks, axis=(1, 3, 5)) * 0.125  22 us
    all_gather x1, blocking collectives, body(): lax.all_gather(coarse_y, 'gx', axis=2, tiled=True)  21.7 us
    all_gather x1, blocking collectives, body(): lax.all_gather(coarse_damp, 'gx', axis=2, tiled=True)  21.7 us
    ppermute x8, starting transfers between devices, extended(): before = lax.ppermute(last, axis, up)  21.6 us
    all_gather x1, blocking collectives, body(): lax.all_gather(coarse_x, 'gx', axis=2, tiled=True)  20.6 us
    ppermute x8, starting transfers between devices, extended(): after = lax.ppermute(leading, axis, down)  19.8 us
  transfers between devices with their start and end apart: 30, of which 15 were waited for; matrix products, arithmetic and copies ran while one was open for 26% of the time, Pallas kernels for 0%

commit v1 on v0

--- a/solution.py
+++ b/solution.py
@@ -5,6 +5,10 @@
 
 COARSE = 3
 RELAX = 0.8
+
+
+def place_the_windows(slab_in, comm_axis, in_dim):
+    return jnp.concatenate(lax.all_gather(slab_in, comm_axis), in_dim)
 
 
 def extended(value, sides, width):
@@ -158,7 +162,7 @@
         lax.all_gather(coarse_residual, "gx", axis=2, tiled=True),
         lax.all_gather(coarse_x, "gx", axis=2, tiled=True),
         lax.all_gather(coarse_y, "gx", axis=2, tiled=True),
-        lax.all_gather(coarse_z, "gx", axis=2, tiled=True),
+        place_the_windows(coarse_z, "gx", 2),
         lax.all_gather(coarse_damp, "gx", axis=2, tiled=True),
     )
     cz_top = top_masked(whole_z)

time: 387 us -> 380 us (0.982)
  blocking collectives: 118 us -> 109 us
    all_gather x1, blocking collectives: 23.2 us -> 14.1 us  [place_the_windows(): return jnp.concatenate(lax.all_gather(slab_in, comm_axis), in_dim)]
where the time goes in v1:
time: 380 us; the launch traced here: 378 us
  blocking collectives  109 us (29%)
  starting transfers between devices  94.9 us (25%)
  local copies, waits for them, and re-layouts  76.8 us (20%)
  other arithmetic  48.9 us (13%)
  waiting for transfers between devices  45.5 us (12%)
    reshape x5, local copies, waits for them, and re-layouts, restrict(): blocks = field.reshape(levels // 2, 2, rows // 2, 2, columns // 2, 2)  48.6 us
    reduce_sum x5, other arithmetic, restrict(): return jnp.sum(blocks, axis=(1, 3, 5)) * 0.125  22 us
    all_gather x1, blocking collectives, body(): lax.all_gather(coarse_y, 'gx', axis=2, tiled=True)  21.7 us
    all_gather x1, blocking collectives, body(): lax.all_gather(coarse_damp, 'gx', axis=2, tiled=True)  21.7 us
    ppermute x8, starting transfers between devices, extended(): before = lax.ppermute(last, axis, up)  21.6 us
    all_gather x1, blocking collectives, body(): lax.all_gather(coarse_x, 'gx', axis=2, tiled=True)  20.6 us
    ppermute x8, starting transfers between devices, extended(): after = lax.ppermute(leading, axis, down)  19.8 us
    all_gather x1, blocking collectives, body(): lax.all_gather(coarse_residual, 'gx', axis=2, tiled=True)  19.2 us
  transfers between devices with their start and end apart: 30, of which 15 were waited for; matrix products, arithmetic and copies ran while one was open for 26% of the time, Pallas kernels for 0%

profile of v1, /device:TPU:4, one launch (start us, length us, event | category | flops | bytes accessed | tf_op | source)
XLA Modules:
  0.0 377.7 jit_solution(6967750471538641045)
XLA Ops:
  0.6 4.9 %all-to-all-start.1 = ((f32[16,16,128]{2,1,0:T(8,128)}), f32[16,16,128]{2,1,0:T(8,128)S(1)}, u32[]{:S(2)}, u32[]{:S(2)}) async-start(f32[16,16,128]{2,1,0:T(8,128)} %param.8), calls=%async_computation.1 | async-start | bytes 262144 | tf_op jit(solution)/shard_map/all_to_all | solution.py:131
  6.4 1.9 collective-permute-start.2
  8.3 4.5 %collective-permute-start.3 = (f32[16,1,128]{2,1,0:T(1,128)S(1)}, f32[16,1,128]{2,1,0:T(1,128)S(1)}, u32[]{:S(2)}, u32[]{:S(2)}) collective-permute-start(f32[16,1,128]{2,1,0:T(1,128)S(1)} %get-tuple-element.266), channel_id=1, source_target_pairs={{1,0},{2,1},{3,2},{4,3},{5,4},{6,5},{7,6},{9,8},{10,9},{11,10},{12... | collective-permute-start | bytes 24584 | tf_op jit(solution)/shard_map/ppermute | solution.py:22
  13.7 1.9 collective-permute-start.1
  16.6 3.9 %collective-permute-start = (f32[16,16,1]{2,1,0:T(8,128)S(1)}, f32[16,16,1]{2,1,0:T(8,128)S(1)}, u32[]{:S(2)}, u32[]{:S(2)}) collective-permute-start(f32[16,16,1]{2,1,0:T(8,128)S(1)} %slice.761), channel_id=1, source_target_pairs={{0,8},{8,16},{16,24},{1,9},{9,17},{17,25},{2,10},{10,18},{18,26},{... | collective-permute-start | bytes 3080 | tf_op jit(solution)/shard_map/ppermute | solution.py:30
  22.6 1.6 collective-permute-done
  24.2 2.2 add_add_fusion
  26.4 11.4 %all_to_all.236 = f32[16,16,128]{2,1,0:T(8,128)S(1)} all-to-all(f32[16,16,128]{2,1,0:T(8,128)S(1)} %get-tuple-element.78), channel_id=1, replica_groups=mesh['gx'=4,'gy'=8] {'gx'}, dimensions={0} | all-to-all | bytes 262144 | tf_op jit(solution)/shard_map/all_to_all | solution.py:129
  37.8 3.3 all-to-all-start.2
  41.4 5.6 %all-to-all-done.2 = f32[16,16,128]{2,1,0:T(8,128)S(1)} async-done(((f32[16,16,128]{2,1,0:T(8,128)}), f32[16,16,128]{2,1,0:T(8,128)S(1)}, u32[]{:S(2)}, u32[]{:S(2)}) %all-to-all-start.2) | async-done | bytes 131104 | tf_op jit(solution)/shard_map/all_to_all | solution.py:130
  47.0 3.3 all-to-all-start.5
  56.6 4.2 %all-to-all-start.6 = ((f32[16,16,128]{2,1,0:T(8,128)}), f32[16,16,128]{2,1,0:T(8,128)S(1)}, u32[]{:S(2)}, u32[]{:S(2)}) async-start(f32[16,16,128]{2,1,0:T(8,128)} %get-tuple-element.76), calls=%async_computation.6 | async-start | bytes 262144 | tf_op jit(solution)/shard_map/all_to_all | solution.py:143
  61.3 1.5 reshape.52
  62.8 2.1 all-to-all-done.6
  64.9 3.3 all-to-all-start.3
  68.2 9.7 %reshape.46 = f32[8,2,8,2,64,2]{5,4,3,2,1,0:T(8,128)} reshape(f32[16,16,128]{2,1,0:T(8,128)S(1)} %copy-done) | data formatting | bytes 262144 | tf_op jit(solution)/shard_map/reshape | solution.py:85
  78.0 4.7 %reduce_sum.47 = f32[8,8,64]{2,1,0:T(8,128)} reduce(f32[8,2,8,2,64,2]{5,4,3,2,1,0:T(8,128)} %reshape.46, f32[]{:T(128)} %constant.7.clone.1), dimensions={1,3,5}, to_apply=%region_2.3 | reduce | flops 28672 | bytes 147460 | tf_op jit(solution)/shard_map/reduce_sum | solution.py:86
  85.5 3.9 %collective-permute-start.4 = (f32[16,16,1]{2,1,0:T(8,128)S(1)}, f32[16,16,1]{2,1,0:T(8,128)S(1)}, u32[]{:S(2)}, u32[]{:S(2)}) collective-permute-start(f32[16,16,1]{2,1,0:T(8,128)S(1)} %get-tuple-element.186), channel_id=1, source_target_pairs={{0,8},{8,16},{16,24},{1,9},{9,17},{17,25},{2,10},{10,18},{18,26},{... | collective-permute-start | bytes 3080 | tf_op jit(solution)/shard_map/ppermute | solution.py:21
  89.4 1.3 collective-permute-start.5
  91.9 4.4 %collective-permute-done.5 = f32[16,16,1]{2,1,0:T(8,128)S(1)} collective-permute-done((f32[16,16,1]{2,1,0:T(8,128)S(1)}, f32[16,16,1]{2,1,0:T(8,128)S(1)}, u32[]{:S(2)}, u32[]{:S(2)}) %collective-permute-start.5) | collective-permute-done | bytes 1056 | tf_op jit(solution)/shard_map/ppermute | solution.py:22
  97.2 4.8 %all-to-all-start.4 = ((f32[16,16,128]{2,1,0:T(8,128)}), f32[16,16,128]{2,1,0:T(8,128)S(1)}, u32[]{:S(2)}, u32[]{:S(2)}) async-start(f32[16,16,128]{2,1,0:T(8,128)} %fusion.22), calls=%async_computation.4 | async-start | bytes 262144 | tf_op jit(solution)/shard_map/all_to_all | solution.py:142
  101.9 4.0 %all-to-all-done.4 = f32[16,16,128]{2,1,0:T(8,128)S(1)} async-done(((f32[16,16,128]{2,1,0:T(8,128)}), f32[16,16,128]{2,1,0:T(8,128)S(1)}, u32[]{:S(2)}, u32[]{:S(2)}) %all-to-all-start.4) | async-done | bytes 131104 | tf_op jit(solution)/shard_map/all_to_all | solution.py:142
  109.9 5.6 %all-to-all-start.7 = ((f32[2,128,128]{2,0,1:T(2,128)}), f32[2,128,128]{2,0,1:T(2,128)}, u32[]{:S(2)}, u32[]{:S(2)}) async-start(f32[2,128,128]{2,0,1:T(2,128)} %copy.196), calls=%async_computation.7 | async-start | bytes 262144 | tf_op jit(solution)/shard_map/all_to_all | solution.py:98
  115.6 21.7 %all_gather.18 = f32[8,8,256]{1,0,2:T(8,128)S(1)} all-gather(f32[8,8,64]{1,0,2:T(8,128)S(1)} %copy.212), channel_id=1, replica_groups=mesh['gx'=4,'gy'=8] {'gx'}, dimensions={2}, use_global_device_ids=true | all-gather | bytes 81920 | tf_op jit(solution)/shard_map/all_gather | solution.py:164
  138.0 2.1 collective-permute-start.14
  140.1 9.7 %reshape.47 = f32[8,2,8,2,64,2]{5,4,3,2,1,0:T(8,128)} reshape(f32[16,16,128]{2,1,0:T(8,128)S(1)} %copy-done.2) | data formatting | bytes 262144 | tf_op jit(solution)/shard_map/reshape | solution.py:85
  149.8 4.0 %reduce_sum.48 = f32[8,8,64]{2,1,0:T(8,128)S(1)} reduce(f32[8,2,8,2,64,2]{5,4,3,2,1,0:T(8,128)} %reshape.47, f32[]{:T(128)} %constant.7.clone.1), dimensions={1,3,5}, to_apply=%region_3.4 | reduce | flops 28672 | bytes 147460 | tf_op jit(solution)/shard_map/reduce_sum | solution.py:86
  154.8 3.5 collective-permute-start.6
  158.3 3.0 collective-permute-start.7
  161.3 1.3 collective-permute-done.7
  163.4 3.3 all-to-all-start.8
  166.7 9.7 %reshape.50 = f32[8,2,8,2,64,2]{5,4,3,2,1,0:T(8,128)} reshape(f32[16,16,128]{2,1,0:T(8,128)S(1)} %copy-done.47) | data formatting | bytes 262144 | tf_op jit(solution)/shard_map/reshape | solution.py:85
  176.4 9.7 %reshape.45 = f32[8,2,8,2,64,2]{5,4,3,2,1,0:T(8,128)} reshape(f32[16,16,128]{2,1,0:T(8,128)S(1)} %copy-done.1) | data formatting | bytes 262144 | tf_op jit(solution)/shard_map/reshape | solution.py:85
  186.1 4.7 %reduce_sum.49 = f32[8,8,64]{2,1,0:T(8,128)} reduce(f32[8,2,8,2,64,2]{5,4,3,2,1,0:T(8,128)} %reshape.50, f32[]{:T(128)} %constant.7.clone.1), dimensions={1,3,5}, to_apply=%region_4.5 | reduce | flops 28672 | bytes 147460 | tf_op jit(solution)/shard_map/reduce_sum | solution.py:86
  190.8 14.1 %all-gather = f32[32,8,64]{2,1,0:T(8,128)S(1)} all-gather(f32[8,8,64]{2,1,0:T(8,128)S(1)} %broadcast_multiply_fusion.1), channel_id=2, replica_groups=mesh['gx'=4,'gy'=8] {'gx'}, dimensions={0}, use_global_device_ids=true | all-gather | bytes 81920 | tf_op jit(solution)/shard_map/all_gather | solution.py:11
  205.7 4.6 %reduce_sum.46 = f32[8,8,64]{2,1,0:T(8,128)} reduce(f32[8,2,8,2,64,2]{5,4,3,2,1,0:T(8,128)} %reshape.45, f32[]{:T(128)} %constant.7.clone.1), dimensions={1,3,5}, to_apply=%region_1.2 | reduce | flops 28672 | bytes 147460 | tf_op jit(solution)/shard_map/reduce_sum | solution.py:86
  218.2 1.5 reshape.54
  219.7 4.6 %all-to-all-start.9 = ((f32[4,1,8192]{2,1,0:T(1,128)}), f32[4,1,8192]{2,1,0:T(1,128)S(1)}, u32[]{:S(2)}, u32[]{:S(2)}) async-start(f32[4,1,8192]{2,1,0:T(1,128)} %reshape.54), calls=%async_computation.9 | async-start | bytes 262144 | tf_op jit(solution)/shard_map/all_to_all | solution.py:94
  224.3 1.5 broadcast_select_fusion.1
  225.9 4.4 %all-to-all-done.9 = f32[4,1,8192]{2,1,0:T(1,128)S(1)} async-done(((f32[4,1,8192]{2,1,0:T(1,128)}), f32[4,1,8192]{2,1,0:T(1,128)S(1)}, u32[]{:S(2)}, u32[]{:S(2)}) %all-to-all-start.9) | async-done | bytes 131104 | tf_op jit(solution)/shard_map/all_to_all | solution.py:94
  232.5 3.3 collective-permute-start.8
  238.3 4.4 %collective-permute-done.9 = f32[16,16,1]{2,1,0:T(8,128)S(1)} collective-permute-done((f32[16,16,1]{2,1,0:T(8,128)S(1)}, f32[16,16,1]{2,1,0:T(8,128)S(1)}, u32[]{:S(2)}, u32[]{:S(2)}) %collective-permute-start.9) | collective-permute-done | bytes 1056 | tf_op jit(solution)/shard_map/ppermute | solution.py:22
  242.7 1.8 fusion.12
  244.4 3.5 all-to-all-start.10
  248.0 1.4 broadcast_multiply_fusion
  249.3 2.4 all-to-all-done.10
  256.9 4.8 %all-to-all-start.11 = ((f32[2,128,128]{2,0,1:T(2,128)}), f32[2,128,128]{2,0,1:T(2,128)S(1)}, u32[]{:S(2)}, u32[]{:S(2)}) async-start(f32[2,128,128]{2,0,1:T(2,128)} %copy.204), calls=%async_computation.11 | async-start | bytes 262144 | tf_op jit(solution)/shard_map/all_to_all | solution.py:98
  263.4 21.7 %all_gather.20 = f32[8,8,256]{1,0,2:T(8,128)S(1)} all-gather(f32[8,8,64]{1,0,2:T(8,128)S(1)} %copy.218), channel_id=1, replica_groups=mesh['gx'=4,'gy'=8] {'gx'}, dimensions={2}, use_global_device_ids=true | all-gather | bytes 81920 | tf_op jit(solution)/shard_map/all_gather | solution.py:166
  285.2 1.9 collective-permute-start.10
  287.1 4.5 %collective-permute-start.11 = (f32[16,1,128]{2,1,0:T(1,128)S(1)}, f32[16,1,128]{2,1,0:T(1,128)S(1)}, u32[]{:S(2)}, u32[]{:S(2)}) collective-permute-start(f32[16,1,128]{2,1,0:T(1,128)S(1)} %get-tuple-element.84), channel_id=1, source_target_pairs={{1,0},{2,1},{3,2},{4,3},{5,4},{6,5},{7,6},{9,8},{10,9},{11,10},{12... | collective-permute-start | bytes 24584 | tf_op jit(solution)/shard_map/ppermute | solution.py:22
  291.7 20.6 %all_gather.17 = f32[8,8,256]{1,0,2:T(8,128)} all-gather(f32[8,8,64]{1,0,2:T(8,128)S(1)} %copy.209), channel_id=1, replica_groups=mesh['gx'=4,'gy'=8] {'gx'}, dimensions={2}, use_global_device_ids=true | all-gather | bytes 81920 | tf_op jit(solution)/shard_map/all_gather | solution.py:163
  313.8 1.5 copy.210
  316.2 2.3 collective-permute-start.12
  319.9 1.8 collective-permute-done.12
  321.7 4.4 %collective-permute-done.13 = f32[16,18,1]{2,1,0:T(8,128)S(1)} collective-permute-done((f32[16,18,1]{2,1,0:T(8,128)S(1)}, f32[16,18,1]{2,1,0:T(8,128)S(1)}, u32[]{:S(2)}, u32[]{:S(2)}) %collective-permute-start.13) | collective-permute-done | bytes 1184 | tf_op jit(solution)/shard_map/ppermute | solution.py:22
  327.3 9.7 %reshape.44 = f32[8,2,8,2,64,2]{5,4,3,2,1,0:T(8,128)} reshape(f32[16,16,128]{2,1,0:T(8,128)S(1)} %fusion.3) | data formatting | bytes 262144 | tf_op jit(solution)/shard_map/reshape | solution.py:85
  337.0 4.0 %reduce_sum.45 = f32[8,8,64]{2,1,0:T(8,128)S(1)} reduce(f32[8,2,8,2,64,2]{5,4,3,2,1,0:T(8,128)} %reshape.44, f32[]{:T(128)} %constant.7.clone.1), dimensions={1,3,5}, to_apply=%region_0.1 | reduce | flops 28672 | bytes 147460 | tf_op jit(solution)/shard_map/reduce_sum | solution.py:86
  341.2 19.2 %all_gather.16 = f32[8,8,256]{1,0,2:T(8,128)S(1)} all-gather(f32[8,8,64]{1,0,2:T(8,128)S(1)} %copy.207), channel_id=1, replica_groups=mesh['gx'=4,'gy'=8] {'gx'}, dimensions={2}, use_global_device_ids=true | all-gather | bytes 81920 | tf_op jit(solution)/shard_map/all_gather | solution.py:162
  361.0 1.9 collective-permute-start.16
  363.0 2.4 collective-permute-start.15
  365.4 3.4 collective-permute-done.15
  369.1 1.9 collective-permute-start.18
  371.0 2.4 collective-permute-start.17
  373.5 3.4 collective-permute-done.17
  (370 shorter events, 48.8 us)
Async XLA Ops:
  0.6 25.7 %all-to-all-start.1 = ((f32[16,16,128]{2,1,0:T(8,128)}), f32[16,16,128]{2,1,0:T(8,128)S(1)}, u32[]{:S(2)}, u32[]{:S(2)}) async-start(f32[16,16,128]{2,1,0:T(8,128)} %param.8), calls=%async_computation.1 | async-start | bytes 262144 | tf_op jit(solution)/shard_map/all_to_all | solution.py:131
  6.4 17.8 %collective-permute-start.2 = (f32[16,1,128]{2,1,0:T(1,128)S(1)}, f32[16,1,128]{2,1,0:T(1,128)S(1)}, u32[]{:S(2)}, u32[]{:S(2)}) collective-permute-start(f32[16,1,128]{2,1,0:T(1,128)S(1)} %get-tuple-element.265), channel_id=1, source_target_pairs={{0,1},{1,2},{2,3},{3,4},{4,5},{5,6},{6,7},{8,9},{9,10},{10,11},{11... | collective-permute-start | bytes 24584 | tf_op jit(solution)/shard_map/ppermute | solution.py:21
  8.3 15.9 %collective-permute-start.3 = (f32[16,1,128]{2,1,0:T(1,128)S(1)}, f32[16,1,128]{2,1,0:T(1,128)S(1)}, u32[]{:S(2)}, u32[]{:S(2)}) collective-permute-start(f32[16,1,128]{2,1,0:T(1,128)S(1)} %get-tuple-element.266), channel_id=1, source_target_pairs={{1,0},{2,1},{3,2},{4,3},{5,4},{6,5},{7,6},{9,8},{10,9},{11,10},{12... | collective-permute-start | bytes 24584 | tf_op jit(solution)/shard_map/ppermute | solution.py:22
  13.7 10.5 %collective-permute-start.1 = (f32[16,1,128]{2,1,0:T(1,128)S(1)}, f32[16,1,128]{2,1,0:T(1,128)S(1)}, u32[]{:S(2)}, u32[]{:S(2)}) collective-permute-start(f32[16,1,128]{2,1,0:T(1,128)S(1)} %slice.763), channel_id=1, source_target_pairs={{0,1},{1,2},{2,3},{3,4},{4,5},{5,6},{6,7},{8,9},{9,10},{10,11},{11... | collective-permute-start | bytes 24584 | tf_op jit(solution)/shard_map/ppermute | solution.py:30
  16.6 7.5 %collective-permute-start = (f32[16,16,1]{2,1,0:T(8,128)S(1)}, f32[16,16,1]{2,1,0:T(8,128)S(1)}, u32[]{:S(2)}, u32[]{:S(2)}) collective-permute-start(f32[16,16,1]{2,1,0:T(8,128)S(1)} %slice.761), channel_id=1, source_target_pairs={{0,8},{8,16},{16,24},{1,9},{9,17},{17,25},{2,10},{10,18},{18,26},{... | collective-permute-start | bytes 3080 | tf_op jit(solution)/shard_map/ppermute | solution.py:30
  26.4 69.9 %copy-start.15 = (f32[16,16,128]{2,1,0:T(8,128)}, f32[16,16,128]{2,1,0:T(8,128)S(1)}, u32[]{:S(2)}) copy-start(f32[16,16,128]{2,1,0:T(8,128)S(1)} %get-tuple-element.77) | copy-start | bytes 393220
  37.8 9.2 %all-to-all-start.2 = ((f32[16,16,128]{2,1,0:T(8,128)}), f32[16,16,128]{2,1,0:T(8,128)S(1)}, u32[]{:S(2)}, u32[]{:S(2)}) async-start(f32[16,16,128]{2,1,0:T(8,128)} %get-tuple-element.76), calls=%async_computation.2 | async-start | bytes 262144 | tf_op jit(solution)/shard_map/all_to_all | solution.py:130
  47.0 9.6 %all-to-all-start.5 = ((f32[16,16,128]{2,1,0:T(8,128)}), f32[16,16,128]{2,1,0:T(8,128)S(1)}, u32[]{:S(2)}, u32[]{:S(2)}) async-start(f32[16,16,128]{2,1,0:T(8,128)} %param.9), calls=%async_computation.5 | async-start | bytes 262144 | tf_op jit(solution)/shard_map/all_to_all | solution.py:144
  55.8 26.8 %copy-start.34 = (f32[4,16,512]{2,1,0:T(8,128)}, f32[4,16,512]{2,1,0:T(8,128)S(1)}, u32[]{:S(2)}) copy-start(f32[4,16,512]{2,1,0:T(8,128)S(1)} %get-tuple-element.40) | copy-start | bytes 393220
  55.8 26.8 %copy-start.41 = (f32[4,16,512]{2,1,0:T(8,128)}, f32[4,16,512]{2,1,0:T(8,128)S(1)}, u32[]{:S(2)}) copy-start(f32[4,16,512]{2,1,0:T(8,128)S(1)} %get-tuple-element.39) | copy-start | bytes 393220
  55.9 26.7 %copy-start.37 = (f32[4,16,512]{2,1,0:T(8,128)}, f32[4,16,512]{2,1,0:T(8,128)S(1)}, u32[]{:S(2)}) copy-start(f32[4,16,512]{2,1,0:T(8,128)S(1)} %get-tuple-element.41) | copy-start | bytes 393220
  56.6 26.1 %copy-start.44 = (f32[4,16,512]{2,1,0:T(8,128)}, f32[4,16,512]{2,1,0:T(8,128)S(1)}, u32[]{:S(2)}) copy-start(f32[4,16,512]{2,1,0:T(8,128)S(1)} %get-tuple-element.190) | copy-start | bytes 393220
  56.6 26.1 %copy-start.57 = (f32[4,16,256]{2,1,0:T(8,128)}, f32[4,16,256]{2,1,0:T(8,128)S(1)}, u32[]{:S(2)}) copy-start(f32[4,16,256]{2,1,0:T(8,128)S(1)} %slice.1048) | copy-start | bytes 196612
  56.6 8.2 %all-to-all-start.6 = ((f32[16,16,128]{2,1,0:T(8,128)}), f32[16,16,128]{2,1,0:T(8,128)S(1)}, u32[]{:S(2)}, u32[]{:S(2)}) async-start(f32[16,16,128]{2,1,0:T(8,128)} %get-tuple-element.76), calls=%async_computation.6 | async-start | bytes 262144 | tf_op jit(solution)/shard_map/all_to_all | solution.py:143
  64.9 17.9 %all-to-all-start.3 = ((f32[4,1,8192]{2,1,0:T(1,128)}), f32[4,1,8192]{2,1,0:T(1,128)S(1)}, u32[]{:S(2)}, u32[]{:S(2)}) async-start(f32[4,1,8192]{2,1,0:T(1,128)} %reshape.52), calls=%async_computation.3 | async-start | bytes 262144 | tf_op jit(solution)/shard_map/all_to_all | solution.py:94
  78.0 18.3 %copy-start.1 = (f32[16,16,128]{2,1,0:T(8,128)S(1)}, f32[16,16,128]{2,1,0:T(8,128)}, u32[]{:S(2)}) copy-start(f32[16,16,128]{2,1,0:T(8,128)} %param.8) | copy-start | bytes 393220
  78.0 18.3 %copy-start.2 = (f32[16,16,128]{2,1,0:T(8,128)S(1)}, f32[16,16,128]{2,1,0:T(8,128)}, u32[]{:S(2)}) copy-start(f32[16,16,128]{2,1,0:T(8,128)} %param.10) | copy-start | bytes 393220
  78.0 18.3 %copy-start.3 = (f32[16,16,128]{2,1,0:T(8,128)S(1)}, f32[16,16,128]{2,1,0:T(8,128)}, u32[]{:S(2)}) copy-start(f32[16,16,128]{2,1,0:T(8,128)} %param.6) | copy-start | bytes 393220
  85.5 6.4 %collective-permute-start.4 = (f32[16,16,1]{2,1,0:T(8,128)S(1)}, f32[16,16,1]{2,1,0:T(8,128)S(1)}, u32[]{:S(2)}, u32[]{:S(2)}) collective-permute-start(f32[16,16,1]{2,1,0:T(8,128)S(1)} %get-tuple-element.186), channel_id=1, source_target_pairs={{0,8},{8,16},{16,24},{1,9},{9,17},{17,25},{2,10},{10,18},{18,26},{... | collective-permute-start | bytes 3080 | tf_op jit(solution)/shard_map/ppermute | solution.py:21
  89.4 6.9 %collective-permute-start.5 = (f32[16,16,1]{2,1,0:T(8,128)S(1)}, f32[16,16,1]{2,1,0:T(8,128)S(1)}, u32[]{:S(2)}, u32[]{:S(2)}) collective-permute-start(f32[16,16,1]{2,1,0:T(8,128)S(1)} %get-tuple-element.187), channel_id=1, source_target_pairs={{8,0},{16,8},{24,16},{9,1},{17,9},{25,17},{10,2},{18,10},{26,18},{... | collective-permute-start | bytes 3080 | tf_op jit(solution)/shard_map/ppermute | solution.py:22
  97.2 8.8 %all-to-all-start.4 = ((f32[16,16,128]{2,1,0:T(8,128)}), f32[16,16,128]{2,1,0:T(8,128)S(1)}, u32[]{:S(2)}, u32[]{:S(2)}) async-start(f32[16,16,128]{2,1,0:T(8,128)} %fusion.22), calls=%async_computation.4 | async-start | bytes 262144 | tf_op jit(solution)/shard_map/all_to_all | solution.py:142
  107.4 42.4 %copy-start.23 = (f32[2,128,128]{2,1,0:T(8,128)}, f32[2,128,128]{2,1,0:T(8,128)S(1)}, u32[]{:S(2)}) copy-start(f32[2,128,128]{2,1,0:T(8,128)S(1)} %get-tuple-element.17) | copy-start | bytes 393220
  109.9 44.0 %all-to-all-start.7 = ((f32[2,128,128]{2,0,1:T(2,128)}), f32[2,128,128]{2,0,1:T(2,128)}, u32[]{:S(2)}, u32[]{:S(2)}) async-start(f32[2,128,128]{2,0,1:T(2,128)} %copy.196), calls=%async_computation.7 | async-start | bytes 262144 | tf_op jit(solution)/shard_map/all_to_all | solution.py:98
  138.0 28.7 %copy-start.47 = (f32[16,16,128]{2,1,0:T(8,128)S(1)}, f32[16,16,128]{2,1,0:T(8,128)}, u32[]{:S(2)}) copy-start(f32[16,16,128]{2,1,0:T(8,128)} %param.11) | copy-start | bytes 393220
  138.0 177.3 %collective-permute-start.14 = (f32[8,1,256]{2,0,1:T(8,128)S(1)}, f32[8,1,256]{2,0,1:T(8,128)}, u32[]{:S(2)}, u32[]{:S(2)}) collective-permute-start(f32[8,1,256]{2,0,1:T(8,128)S(1)} %copy.213), channel_id=1, source_target_pairs={{0,1},{1,2},{2,3},{3,4},{4,5},{5,6},{6,7},{8,9},{9,10},{10,11},{11... | collective-permute-start | bytes 24584 | tf_op jit(solution)/shard_map/ppermute | solution.py:30
  154.8 6.5 %collective-permute-start.6 = (f32[16,1,128]{2,1,0:T(1,128)S(1)}, f32[16,1,128]{2,1,0:T(1,128)S(1)}, u32[]{:S(2)}, u32[]{:S(2)}) collective-permute-start(f32[16,1,128]{2,1,0:T(1,128)S(1)} %get-tuple-element.123), channel_id=1, source_target_pairs={{0,1},{1,2},{2,3},{3,4},{4,5},{5,6},{6,7},{8,9},{9,10},{10,11},{11... | collective-permute-start | bytes 24584 | tf_op jit(solution)/shard_map/ppermute | solution.py:21
  158.3 4.3 %collective-permute-start.7 = (f32[16,1,128]{2,1,0:T(1,128)S(1)}, f32[16,1,128]{2,1,0:T(1,128)S(1)}, u32[]{:S(2)}, u32[]{:S(2)}) collective-permute-start(f32[16,1,128]{2,1,0:T(1,128)S(1)} %get-tuple-element.124), channel_id=1, source_target_pairs={{1,0},{2,1},{3,2},{4,3},{5,4},{6,5},{7,6},{9,8},{10,9},{11,10},{12... | collective-permute-start | bytes 24584 | tf_op jit(solution)/shard_map/ppermute | solution.py:22
  163.4 47.0 %all-to-all-start.8 = ((f32[16,16,128]{2,1,0:T(8,128)}), f32[16,16,128]{2,1,0:T(8,128)S(1)}, u32[]{:S(2)}, u32[]{:S(2)}) async-start(f32[16,16,128]{2,1,0:T(8,128)} %fusion.17), calls=%async_computation.8 | async-start | bytes 262144 | tf_op jit(solution)/shard_map/all_to_all | solution.py:129
  186.1 26.1 %copy-start.25 = (f32[4,16,512]{2,1,0:T(8,128)S(1)}, f32[4,16,512]{2,1,0:T(8,128)}, u32[]{:S(2)}) copy-start(f32[4,16,512]{2,1,0:T(8,128)} %copy-done.24) | copy-start | bytes 393220
  186.1 26.1 %copy-start.27 = (f32[4,16,512]{2,1,0:T(8,128)S(1)}, f32[4,16,512]{2,1,0:T(8,128)}, u32[]{:S(2)}) copy-start(f32[4,16,512]{2,1,0:T(8,128)} %copy-done.26) | copy-start | bytes 393220
  190.8 22.1 %copy-start.6 = (f32[4,16,512]{2,1,0:T(8,128)S(1)}, f32[4,16,512]{2,1,0:T(8,128)}, u32[]{:S(2)}) copy-start(f32[4,16,512]{2,1,0:T(8,128)} %copy-done.5) | copy-start | bytes 393220
  190.8 22.3 %copy-start.8 = (f32[4,16,512]{2,1,0:T(8,128)S(1)}, f32[4,16,512]{2,1,0:T(8,128)}, u32[]{:S(2)}) copy-start(f32[4,16,512]{2,1,0:T(8,128)} %copy-done.7) | copy-start | bytes 393220
  190.8 22.3 %copy-start.10 = (f32[4,16,512]{2,1,0:T(8,128)S(1)}, f32[4,16,512]{2,1,0:T(8,128)}, u32[]{:S(2)}) copy-start(f32[4,16,512]{2,1,0:T(8,128)} %copy-done.9) | copy-start | bytes 393220
  190.8 22.5 %copy-start.22 = (f32[4,16,512]{2,1,0:T(8,128)S(1)}, f32[4,16,512]{2,1,0:T(8,128)}, u32[]{:S(2)}) copy-start(f32[4,16,512]{2,1,0:T(8,128)} %copy-done.21) | copy-start | bytes 393220
  212.8 39.0 %copy-start.29 = (f32[2,128,128]{2,1,0:T(8,128)S(1)}, f32[2,128,128]{2,1,0:T(8,128)}, u32[]{:S(2)}) copy-start(f32[2,128,128]{2,1,0:T(8,128)} %copy-done.28) | copy-start | bytes 393220
  213.0 39.8 %copy-start.12 = (f32[2,128,128]{2,1,0:T(8,128)S(1)}, f32[2,128,128]{2,1,0:T(8,128)}, u32[]{:S(2)}) copy-start(f32[2,128,128]{2,1,0:T(8,128)} %copy-done.11) | copy-start | bytes 393220
  213.0 39.8 %copy-start.14 = (f32[2,128,128]{2,1,0:T(8,128)S(1)}, f32[2,128,128]{2,1,0:T(8,128)}, u32[]{:S(2)}) copy-start(f32[2,128,128]{2,1,0:T(8,128)} %copy-done.13) | copy-start | bytes 393220
  213.2 39.7 %copy-start.18 = (f32[2,128,128]{2,1,0:T(8,128)S(1)}, f32[2,128,128]{2,1,0:T(8,128)}, u32[]{:S(2)}) copy-start(f32[2,128,128]{2,1,0:T(8,128)} %copy-done.17) | copy-start | bytes 393220
  213.2 39.7 %copy-start.20 = (f32[2,128,128]{2,1,0:T(8,128)S(1)}, f32[2,128,128]{2,1,0:T(8,128)}, u32[]{:S(2)}) copy-start(f32[2,128,128]{2,1,0:T(8,128)} %copy-done.19) | copy-start | bytes 393220
  219.7 10.6 %all-to-all-start.9 = ((f32[4,1,8192]{2,1,0:T(1,128)}), f32[4,1,8192]{2,1,0:T(1,128)S(1)}, u32[]{:S(2)}, u32[]{:S(2)}) async-start(f32[4,1,8192]{2,1,0:T(1,128)} %reshape.54), calls=%async_computation.9 | async-start | bytes 262144 | tf_op jit(solution)/shard_map/all_to_all | solution.py:94
  232.3 21.7 %copy-start.50 = (f32[2,128,128]{2,1,0:T(8,128)S(1)}, f32[2,128,128]{2,1,0:T(8,128)}, u32[]{:S(2)}) copy-start(f32[2,128,128]{2,1,0:T(8,128)} %copy-done.49) | copy-start | bytes 393220
  232.3 22.7 %copy-start.36 = (f32[2,128,128]{2,1,0:T(8,128)S(1)}, f32[2,128,128]{2,1,0:T(8,128)}, u32[]{:S(2)}) copy-start(f32[2,128,128]{2,1,0:T(8,128)} %copy-done.35) | copy-start | bytes 393220
  232.3 22.7 %copy-start.55 = (f32[2,128,128]{2,1,0:T(8,128)S(1)}, f32[2,128,128]{2,1,0:T(8,128)}, u32[]{:S(2)}) copy-start(f32[2,128,128]{2,1,0:T(8,128)} %copy-done.54) | copy-start | bytes 393220
  232.3 22.8 %copy-start.39 = (f32[2,128,128]{2,1,0:T(8,128)S(1)}, f32[2,128,128]{2,1,0:T(8,128)}, u32[]{:S(2)}) copy-start(f32[2,128,128]{2,1,0:T(8,128)} %copy-done.38) | copy-start | bytes 393220
  232.3 22.8 %copy-start.43 = (f32[2,128,128]{2,1,0:T(8,128)S(1)}, f32[2,128,128]{2,1,0:T(8,128)}, u32[]{:S(2)}) copy-start(f32[2,128,128]{2,1,0:T(8,128)} %copy-done.42) | copy-start | bytes 393220
  232.3 22.8 %copy-start.46 = (f32[2,128,128]{2,1,0:T(8,128)S(1)}, f32[2,128,128]{2,1,0:T(8,128)}, u32[]{:S(2)}) copy-start(f32[2,128,128]{2,1,0:T(8,128)} %copy-done.45) | copy-start | bytes 393220
  232.4 22.8 %copy-start.59 = (f32[2,64,128]{2,1,0:T(8,128)S(1)}, f32[2,64,128]{2,1,0:T(8,128)}, u32[]{:S(2)}) copy-start(f32[2,64,128]{2,1,0:T(8,128)} %copy-done.58) | copy-start | bytes 196612
  232.4 22.8 %copy-start.61 = (f32[2,64,128]{2,1,0:T(8,128)S(1)}, f32[2,64,128]{2,1,0:T(8,128)}, u32[]{:S(2)}) copy-start(f32[2,64,128]{2,1,0:T(8,128)} %copy-done.60) | copy-start | bytes 196612
  232.5 5.8 %collective-permute-start.8 = (f32[16,16,1]{2,1,0:T(8,128)S(1)}, f32[16,16,1]{2,1,0:T(8,128)S(1)}, u32[]{:S(2)}, u32[]{:S(2)}) collective-permute-start(f32[16,16,1]{2,1,0:T(8,128)S(1)} %get-tuple-element.101), channel_id=1, source_target_pairs={{0,8},{8,16},{16,24},{1,9},{9,17},{17,25},{2,10},{10,18},{18,26},{... | collective-permute-start | bytes 3080 | tf_op jit(solution)/shard_map/ppermute | solution.py:21
  235.8 6.9 %collective-permute-start.9 = (f32[16,16,1]{2,1,0:T(8,128)S(1)}, f32[16,16,1]{2,1,0:T(8,128)S(1)}, u32[]{:S(2)}, u32[]{:S(2)}) collective-permute-start(f32[16,16,1]{2,1,0:T(8,128)S(1)} %get-tuple-element.102), channel_id=1, source_target_pairs={{8,0},{16,8},{24,16},{9,1},{17,9},{25,17},{10,2},{18,10},{26,18},{... | collective-permute-start | bytes 3080 | tf_op jit(solution)/shard_map/ppermute | solution.py:22
  244.4 7.3 %all-to-all-start.10 = ((f32[16,16,128]{2,1,0:T(8,128)}), f32[16,16,128]{2,1,0:T(8,128)S(1)}, u32[]{:S(2)}, u32[]{:S(2)}) async-start(f32[16,16,128]{2,1,0:T(8,128)} %fusion.12), calls=%async_computation.10 | async-start | bytes 262144 | tf_op jit(solution)/shard_map/all_to_all | solution.py:142
  252.8 73.4 %copy-start.16 = (f32[16,16,128]{2,1,0:T(8,128)S(1)}, f32[16,16,128]{2,1,0:T(8,128)}, u32[]{:S(2)}) copy-start(f32[16,16,128]{2,1,0:T(8,128)} %copy-done.15) | copy-start | bytes 393220
  256.9 28.3 %all-to-all-start.11 = ((f32[2,128,128]{2,0,1:T(2,128)}), f32[2,128,128]{2,0,1:T(2,128)S(1)}, u32[]{:S(2)}, u32[]{:S(2)}) async-start(f32[2,128,128]{2,0,1:T(2,128)} %copy.204), calls=%async_computation.11 | async-start | bytes 262144 | tf_op jit(solution)/shard_map/all_to_all | solution.py:98
  285.1 51.9 %copy-start.4 = (f32[8,2,16,128]{3,2,1,0:T(8,128)}, f32[8,2,16,128]{3,2,1,0:T(8,128)S(1)}, u32[]{:S(2)}) copy-start(f32[8,2,16,128]{3,2,1,0:T(8,128)S(1)} %copy.206) | copy-start | bytes 393220
  285.2 30.9 %collective-permute-start.10 = (f32[16,1,128]{2,1,0:T(1,128)S(1)}, f32[16,1,128]{2,1,0:T(1,128)S(1)}, u32[]{:S(2)}, u32[]{:S(2)}) collective-permute-start(f32[16,1,128]{2,1,0:T(1,128)S(1)} %get-tuple-element.83), channel_id=1, source_target_pairs={{0,1},{1,2},{2,3},{3,4},{4,5},{5,6},{6,7},{8,9},{9,10},{10,11},{11... | collective-permute-start | bytes 24584 | tf_op jit(solution)/shard_map/ppermute | solution.py:21
  287.1 29.0 %collective-permute-start.11 = (f32[16,1,128]{2,1,0:T(1,128)S(1)}, f32[16,1,128]{2,1,0:T(1,128)S(1)}, u32[]{:S(2)}, u32[]{:S(2)}) collective-permute-start(f32[16,1,128]{2,1,0:T(1,128)S(1)} %get-tuple-element.84), channel_id=1, source_target_pairs={{1,0},{2,1},{3,2},{4,3},{5,4},{6,5},{7,6},{9,8},{10,9},{11,10},{12... | collective-permute-start | bytes 24584 | tf_op jit(solution)/shard_map/ppermute | solution.py:22
  316.2 5.5 %collective-permute-start.12 = (f32[16,18,1]{2,1,0:T(8,128)S(1)}, f32[16,18,1]{2,1,0:T(8,128)S(1)}, u32[]{:S(2)}, u32[]{:S(2)}) collective-permute-start(f32[16,18,1]{2,1,0:T(8,128)S(1)} %get-tuple-element.79), channel_id=1, source_target_pairs={{0,8},{8,16},{16,24},{1,9},{9,17},{17,25},{2,10},{10,18},{18,26},{... | collective-permute-start | bytes 3464 | tf_op jit(solution)/shard_map/ppermute | solution.py:21
  318.5 7.6 %collective-permute-start.13 = (f32[16,18,1]{2,1,0:T(8,128)S(1)}, f32[16,18,1]{2,1,0:T(8,128)S(1)}, u32[]{:S(2)}, u32[]{:S(2)}) collective-permute-start(f32[16,18,1]{2,1,0:T(8,128)S(1)} %get-tuple-element.80), channel_id=1, source_target_pairs={{8,0},{16,8},{24,16},{9,1},{17,9},{25,17},{10,2},{18,10},{26,18},{... | collective-permute-start | bytes 3464 | tf_op jit(solution)/shard_map/ppermute | solution.py:22
  327.3 33.5 %copy-start.40 = (f32[8,8,256]{2,1,0:T(8,128)S(1)}, f32[8,8,256]{2,1,0:T(8,128)}, u32[]{:S(2)}) copy-start(f32[8,8,256]{2,1,0:T(8,128)} %reshape.49) | copy-start | bytes 196612
  341.0 36.6 %copy-start.69 = (f32[8,8,64]{2,1,0:T(8,128)}, f32[8,8,64]{2,1,0:T(8,128)S(1)}, u32[]{:S(2)}) copy-start(f32[8,8,64]{2,1,0:T(8,128)S(1)} %broadcast_multiply_fusion.4) | copy-start | bytes 49156
  361.0 4.4 %collective-permute-start.16 = (f32[8,1,256]{2,0,1:T(8,128)S(1)}, f32[8,1,256]{2,0,1:T(8,128)S(1)}, u32[]{:S(2)}, u32[]{:S(2)}) collective-permute-start(f32[8,1,256]{2,0,1:T(8,128)S(1)} %copy.223), channel_id=1, source_target_pairs={{1,0},{2,1},{3,2},{4,3},{5,4},{6,5},{7,6},{9,8},{10,9},{11,10},{12... | collective-permute-start | bytes 24584 | tf_op jit(solution)/shard_map/ppermute | solution.py:22
  363.0 5.9 %collective-permute-start.15 = (f32[8,1,256]{2,0,1:T(8,128)S(1)}, f32[8,1,256]{2,0,1:T(8,128)S(1)}, u32[]{:S(2)}, u32[]{:S(2)}) collective-permute-start(f32[8,1,256]{2,0,1:T(8,128)S(1)} %copy.221), channel_id=1, source_target_pairs={{0,1},{1,2},{2,3},{3,4},{4,5},{5,6},{6,7},{8,9},{9,10},{10,11},{11... | collective-permute-start | bytes 24584 | tf_op jit(solution)/shard_map/ppermute | solution.py:21
  369.1 4.4 %collective-permute-start.18 = (f32[8,1,256]{2,0,1:T(8,128)S(1)}, f32[8,1,256]{2,0,1:T(8,128)S(1)}, u32[]{:S(2)}, u32[]{:S(2)}) collective-permute-start(f32[8,1,256]{2,0,1:T(8,128)S(1)} %copy.230), channel_id=1, source_target_pairs={{1,0},{2,1},{3,2},{4,3},{5,4},{6,5},{7,6},{9,8},{10,9},{11,10},{12... | collective-permute-start | bytes 24584 | tf_op jit(solution)/shard_map/ppermute | solution.py:22
  371.0 5.9 %collective-permute-start.17 = (f32[8,1,256]{2,0,1:T(8,128)S(1)}, f32[8,1,256]{2,0,1:T(8,128)S(1)}, u32[]{:S(2)}, u32[]{:S(2)}) collective-permute-start(f32[8,1,256]{2,0,1:T(8,128)S(1)} %copy.228), channel_id=1, source_target_pairs={{0,1},{1,2},{2,3},{3,4},{4,5},{5,6},{6,7},{8,9},{9,10},{10,11},{11... | collective-permute-start | bytes 24584 | tf_op jit(solution)/shard_map/ppermute | solution.py:21
  (36 other events, 170.1 us)
